TPU v7x, 256 devices: a whole 4x4x8 slice. The times are simulated.
256 devices in a mesh: row: 32 (over z, x), layer: 8 (over y, core).
Axes of the slice: x: 4, y: 4, z: 8, core: 2. Of those that a mesh axis runs over, the one named last changes fastest.
Arguments:
- window_points: int32 [2, 32768], P(None, 'row'), may hold values from 0 to 63
- pivot_points: int32 [2, 512], replicated, may hold values from 0 to 63
- window_factor: bfloat16 [32768, 16384], P('row', 'layer'), may hold values from -1.5 to 1.5
- pivot_factor: bfloat16 [512, 16384], P('row', 'layer'), may hold values from -0.0234375 to 0.0234375
- right_sides: bfloat16 [32768, 512], P('row', 'layer'), may hold values from -6 to 6
- pivot_sides: bfloat16 [512, 512], P('row', 'layer'), may hold values from -6 to 6
Outputs:
- panel_factor: float32 [32768, 512], P('row', 'layer')
- eliminated: float32 [32768, 512], P('row', 'layer')
All inputs are finite; a program needn't handle non-finite values.
Results may differ from a plain program's by a relative error of at most 0.0006.
Values may be sent and summed in bfloat16 or wider, within the bound.
No kernel may reach another device: no remote copies, remote signals or barrier semaphores. Data moves between devices by JAX's collectives and lax.ppermute only.
A program may use at most 64 MiB of HBM per device.

v0:
```python
import jax
import jax.numpy as jnp
from jax import lax
from jax.sharding import PartitionSpec as P

nugget_value = 2.0
variance_value = 4.0
length_scale = 4.0


def matern(first_points, second_points):
    first_float = first_points.astype(jnp.float32)
    second_float = second_points.astype(jnp.float32)
    delta_x = first_float[0][:, None] - second_float[0][None, :]
    delta_y = first_float[1][:, None] - second_float[1][None, :]
    scaled = jnp.sqrt(delta_x * delta_x + delta_y * delta_y) * (jnp.sqrt(3.0) / length_scale)
    return variance_value * (1.0 + scaled) * jnp.exp(-scaled)


def solvers(factor):

    def right_solve(matrix):
        return jax.scipy.linalg.solve_triangular(factor, matrix.T, lower=True).T

    def left_solve(matrix):
        return jax.scipy.linalg.solve_triangular(factor, matrix, lower=True)

    return (right_solve, left_solve)


def shards(window_points, pivot_points, window_factor, pivot_factor, right_sides, pivot_sides):
    pivots, pivot_block = (
        lax.all_gather(pivot_factor, "row", axis=0, tiled=True),
        lax.all_gather(pivot_sides, "row", axis=0, tiled=True),
    )
    contract = (((1,), (1,)), ((), ()))
    partial_value = lax.dot_general(
        window_factor, pivots, contract, preferred_element_type=jnp.float32
    )
    gram_part = lax.dot_general(pivots, pivots, contract, preferred_element_type=jnp.float32)
    count = pivots.shape[0]
    cov_diagonal = matern(pivot_points, pivot_points) + nugget_value * jnp.eye(
        count, dtype=jnp.float32
    )
    layers = lax.axis_size("layer")
    layer_index = lax.axis_index("layer")
    cov_panel = matern(window_points, pivot_points)
    schur_sum, gram_sum = lax.psum((partial_value, gram_part), "layer")
    factor = jnp.linalg.cholesky(cov_diagonal - gram_sum)
    right_solve, left_solve = solvers(factor)
    solved = right_solve(cov_panel - schur_sum)
    reduced = left_solve(pivot_block.astype(jnp.float32))
    eliminated = right_sides.astype(jnp.float32) - jnp.dot(
        solved, reduced, precision=lax.Precision.HIGHEST
    )
    width = count // layers
    panel_out = lax.dynamic_slice_in_dim(solved, layer_index * width, width, 1)
    return (panel_out, eliminated)


def solution(mesh):
    placed = (
        P(None, "row"),
        P(),
        P("row", "layer"),
        P("row", "layer"),
        P("row", "layer"),
        P("row", "layer"),
    )
    return jax.shard_map(
        shards,
        mesh=mesh,
        in_specs=placed,
        out_specs=(P("row", "layer"), P("row", "layer")),
        check_vma=False,
    )
```

profile of v0, /device:TPU:2, one launch (start us, length us, event | category | flops | bytes accessed | tf_op | source)
XLA Modules:
  0.0 346.6 jit_solution(16420953489318087059)
XLA Ops:
  7.9 82.2 %all-gather.2.cloned.1.call-done = bf16[512,2048]{1,0:T(8,128)(2,1)} async-done(((bf16[16,2048]{1,0:T(8,128)(2,1)}), bf16[512,2048]{1,0:T(8,128)(2,1)}) %all-gather.2.cloned.1.call-update) | async-done | bytes 2097168 | tf_op jit(solution)/shard_map/all_gather | solution.py:33
  90.2 4.6 %fusion.63 = f32[512,512]{0,1:T(8,128)} fusion(bf16[512,2048]{1,0:T(8,128)(2,1)} %all-gather.2.cloned.1.call-done), kind=kOutput, calls=%fused_computation.104 | convolution fusion | flops 1073741824 | bytes 3145728 | tf_op jit(solution)/shard_map/dot_general | solution.py:40
  94.8 3.7 %fusion.64 = f32[1024,512]{1,0:T(8,128)} fusion(bf16[1024,2048]{1,0:T(8,128)(2,1)S(1)} %copy-done.4, bf16[512,2048]{1,0:T(8,128)(2,1)S(1)} %copy-done.5), kind=kOutput, calls=%fused_computation.105 | convolution fusion | flops 2147483648 | bytes 8388608 | tf_op jit(solution)/shard_map/dot_general | solution.py:37
  99.2 42.2 %all_gather.7 = bf16[512,64]{1,0:T(8,128)(2,1)S(1)} all-gather(bf16[16,64]{1,0:T(8,128)(2,1)S(1)} %copy-done.2), channel_id=1, replica_groups=mesh['row'=32,'layer'=8] {'row'}, dimensions={0}, use_global_device_ids=true | all-gather | bytes 67584 | tf_op jit(solution)/shard_map/all_gather | solution.py:34
  141.9 29.5 %all-reduce.4.cloned.1.call-done = (f32[1024,512]{1,0:T(8,128)}, f32[512,512]{0,1:T(8,128)}) async-done(((f32[1024,512]{1,0:T(8,128)}, f32[512,512]{0,1:T(8,128)}), (f32[1024,512]{1,0:T(8,128)}, f32[512,512]{0,1:T(8,128)})) %all-reduce.4.cloned.1.call-update) | async-done | bytes 3145744 | tf_op jit(solution)/shard_map/psum | solution.py:48
  171.5 2.1 add_subtract_fusion
  174.8 11.7 %cholesky.103 = f32[128,128]{1,0:T(8,128)S(1)} custom-call(f32[128,128]{1,0:T(8,128)S(1)} %cholesky.263), custom_call_target="Cholesky" | custom-call | tf_op jit(solution)/shard_map/jit(cholesky)/cholesky | solution.py:49
  186.6 9.8 %custom-call.34 = f32[1,128,128]{1,2,0:T(8,128)S(1)} custom-call(f32[1,128,128]{2,1,0:T(8,128)S(1)} %get-tuple-element.31), custom_call_target="InvertDiagBlocksLowerTriangular" | custom-call | tf_op jit(solution)/shard_map/jit(cholesky)/cholesky | solution.py:49
  197.1 23.5 %cholesky.215 = f32[128,128]{1,0:T(8,128)S(1)} custom-call(f32[128,128]{1,0:T(8,128)S(1)} %cholesky.267), custom_call_target="Cholesky" | custom-call | tf_op jit(solution)/shard_map/jit(cholesky)/cholesky | solution.py:49
  220.9 9.8 %custom-call.35 = f32[1,128,128]{1,2,0:T(8,128)S(1)} custom-call(f32[1,128,128]{2,1,0:T(8,128)S(1)} %get-tuple-element.29), custom_call_target="InvertDiagBlocksLowerTriangular" | custom-call | tf_op jit(solution)/shard_map/jit(cholesky)/cholesky | solution.py:49
  231.8 11.7 %cholesky.236 = f32[128,128]{1,0:T(8,128)S(1)} custom-call(f32[128,128]{1,0:T(8,128)S(1)} %cholesky.272), custom_call_target="Cholesky" | custom-call | tf_op jit(solution)/shard_map/jit(cholesky)/cholesky | solution.py:49
  243.7 9.8 %custom-call.36 = f32[1,128,128]{1,2,0:T(8,128)S(1)} custom-call(f32[1,128,128]{2,1,0:T(8,128)S(1)} %get-tuple-element.27), custom_call_target="InvertDiagBlocksLowerTriangular" | custom-call | tf_op jit(solution)/shard_map/jit(cholesky)/cholesky | solution.py:49
  254.3 11.7 %cholesky.253 = f32[128,128]{1,0:T(8,128)S(1)} custom-call(f32[128,128]{1,0:T(8,128)S(1)} %convolution_subtract_fusion.8), custom_call_target="Cholesky" | custom-call | tf_op jit(solution)/shard_map/jit(cholesky)/cholesky | solution.py:49
  271.3 10.7 %while.1 = (s32[]{:T(128)}, f32[512,512]{0,1:T(8,128)S(1)}, s32[4,2]{0,1:T(2,128)S(1)}, f32[4,128,128]{2,1,0:T(8,128)}, s32[]{:T(128)}) while((s32[]{:T(128)}, f32[512,512]{0,1:T(8,128)S(1)}, s32[4,2]{0,1:T(2,128)S(1)}, f32[4,128,128]{2,1,0:T(8,128)}, s32[]{:T(128)}) %tuple.30), condition=%wide.while_cond, body=%wide.while_body.sunk | while | flops 2 | bytes 393829 | solution.py:23
  271.9 1.3 dynamic-slice.12
  274.5 1.3 dynamic-slice.12
  277.2 1.3 dynamic-slice.12
  279.9 1.3 dynamic-slice.12
  282.0 40.3 %custom-call.37 = f32[4,128,128]{1,2,0:T(8,128)S(1)} custom-call(f32[4,128,128]{2,1,0:T(8,128)} %get-tuple-element.9), custom_call_target="InvertDiagBlocksLowerTriangular" | custom-call | tf_op jit(solution)/shard_map/jit(_solve_triangular)/triangular_solve | solution.py:23
  324.5 3.0 subtract_bitcast_fusion
  328.2 1.0 convolution_subtract_fusion.1
  329.8 1.8 convolution_subtract_fusion
  332.3 2.7 fusion.6
  336.6 2.2 convolution_subtract_fusion.2
  (84 shorter events, 20.8 us)
Async XLA Ops:
  7.2 83.0 %all-gather.2.cloned.1.call-start = ((), (), s32[]{:S(2)}) async-start(), calls=%async_computation | async-start | bytes 2162688 | tf_op jit(solution)/shard_map/all_gather | solution.py:33
  7.9 163.6 %all-reduce.4.cloned.1.call-start = ((), (), s32[]{:S(2)}) async-start(), calls=%async_computation.1 | async-start | bytes 6291456 | tf_op jit(solution)/shard_map/psum | solution.py:48
  90.2 4.6 %copy-start.4 = (bf16[1024,2048]{1,0:T(8,128)(2,1)S(1)}, bf16[1024,2048]{1,0:T(8,128)(2,1)}, u32[]{:S(2)}) copy-start(bf16[1024,2048]{1,0:T(8,128)(2,1)} %param.8) | copy-start | bytes 12582916
  90.2 4.6 %copy-start.5 = (bf16[512,2048]{1,0:T(8,128)(2,1)S(1)}, bf16[512,2048]{1,0:T(8,128)(2,1)}, u32[]{:S(2)}) copy-start(bf16[512,2048]{1,0:T(8,128)(2,1)} %all-gather.2.cloned.1.call-done) | copy-start | bytes 6291460
  98.5 0.7 copy-start.3
  98.5 0.7 copy-start.2
  98.5 42.9 %copy-start.1 = (s32[2,1024]{1,0:T(2,128)S(1)}, s32[2,1024]{1,0:T(2,128)}, u32[]{:S(2)}) copy-start(s32[2,1024]{1,0:T(2,128)} %param.6) | copy-start | bytes 24580
  171.5 2.4 copy-start
  335.7 0.9 copy-start.6
Sparse Core Ops, SparseCore 0:
  10.6 79.5 all-gather.1
  98.6 72.8 all-reduce.3
where the time goes:
time: 350 us; the launch traced here: 347 us
  other arithmetic  137 us (39%)
  waiting for transfers between devices  112 us (32%)
  blocking collectives  42.2 us (12%)
  matrix products  23.1 us (7%)
  between operations  17 us (5%)
  local copies, waits for them, and re-layouts  14.3 us (4%)
    another operation x14, other arithmetic, shards(): factor = jnp.linalg.cholesky(cov_diagonal - gram_sum)  90.2 us
    all_gather x1, waiting for transfers between devices, shards(): lax.all_gather(pivot_factor, 'row', axis=0, tiled=True)  82.2 us
    all_gather x1, blocking collectives, shards(): lax.all_gather(pivot_sides, 'row', axis=0, tiled=True)  42.2 us
    another operation x4, other arithmetic, right_solve(): return jax.scipy.linalg.solve_triangular(factor, matrix.T, lower=True).T  41.2 us
    psum x1, waiting for transfers between devices, shards(): schur_sum, gram_sum = lax.psum((partial_value, gram_part), 'layer')  29.5 us
    another operation x20, local copies, waits for them, and re-layouts  10.6 us
    another operation x7, matrix products, right_solve(): return jax.scipy.linalg.solve_triangular(factor, matrix.T, lower=True).T  8.15 us
  transfers between devices with their start and end apart: 2, of which 2 were waited for; matrix products, arithmetic and copies ran while one was open for 0% of the time, Pallas kernels for 0%

commit v1 on v0

--- a/solution.py
+++ b/solution.py
@@ -31,7 +31,9 @@
 def shards(window_points, pivot_points, window_factor, pivot_factor, right_sides, pivot_sides):
     pivots, pivot_block = (
         lax.all_gather(pivot_factor, "row", axis=0, tiled=True),
-        lax.all_gather(pivot_sides, "row", axis=0, tiled=True),
+        jnp.concatenate(
+            lax.all_to_all(jnp.stack([pivot_sides] * lax.axis_size("row")), "row", 0, 0), axis=0
+        ),
     )
     contract = (((1,), (1,)), ((), ()))
     partial_value = lax.dot_general(

time: 350 us -> 349 us (level)
  blocking collectives: 42.2 us -> 0 us
  waiting for transfers between devices: 112 us -> 147 us
  starting transfers between devices: 0.08 us -> 7.77 us
    all_gather x1 -> x0, blocking collectives: 42.2 us -> none  [shards(): lax.all_gather(pivot_sides, 'row', axis=0, tiled=True)]
    psum x1, waiting for transfers between devices: 29.5 us -> 55.4 us  [shards(): schur_sum, gram_sum = lax.psum((partial_value, gram_part), 'layer')]
    all_to_all x0 -> x1, waiting for transfers between devices: none -> 8.22 us  [shards(): lax.all_to_all(jnp.stack([pivot_sides] * lax.axis_size('row')), 'row', 0, 0)]
    all_to_all x0 -> x1, starting transfers between devices: none -> 7.7 us  [shards(): lax.all_to_all(jnp.stack([pivot_sides] * lax.axis_size('row')), 'row', 0, 0)]
    another operation x20 -> x24, local copies, waits for them, and re-layouts: 10.6 us -> 10.5 us
  transfers between devices with their start and end apart: 2 -> 3, of which waited for: 2 -> 3; matrix products, arithmetic and copies ran while one was open for 0% -> 0% of each run, Pallas kernels for 0% -> 0%
where the time goes in v1:
time: 349 us; the launch traced here: 346 us
  waiting for transfers between devices  147 us (42%)
  other arithmetic  137 us (39%)
  matrix products  23.1 us (7%)
  between operations  17.1 us (5%)
  local copies, waits for them, and re-layouts  14.5 us (4%)
  starting transfers between devices  7.77 us (2%)
    another operation x14, other arithmetic, shards(): factor = jnp.linalg.cholesky(cov_diagonal - gram_sum)  89.9 us
    all_gather x1, waiting for transfers between devices, shards(): lax.all_gather(pivot_factor, 'row', axis=0, tiled=True)  82.3 us
    psum x1, waiting for transfers between devices, shards(): schur_sum, gram_sum = lax.psum((partial_value, gram_part), 'layer')  55.4 us
    another operation x4, other arithmetic, right_solve(): return jax.scipy.linalg.solve_triangular(factor, matrix.T, lower=True).T  40.7 us
    another operation x20, local copies, waits for them, and re-layouts  10.5 us
    all_to_all x1, waiting for transfers between devices, shards(): lax.all_to_all(jnp.stack([pivot_sides] * lax.axis_size('row')), 'row', 0, 0)  8.22 us
    another operation x7, matrix products, right_solve(): return jax.scipy.linalg.solve_triangular(factor, matrix.T, lower=True).T  8.18 us
    all_to_all x1, starting transfers between devices, shards(): lax.all_to_all(jnp.stack([pivot_sides] * lax.axis_size('row')), 'row', 0, 0)  7.7 us
  transfers between devices with their start and end apart: 3, of which 3 were waited for; matrix products, arithmetic and copies ran while one was open for 0% of the time, Pallas kernels for 0%

profile of v1, /device:TPU:2, one launch (start us, length us, event | category | flops | bytes accessed | tf_op | source)
XLA Modules:
  0.0 345.7 jit_solution(3637526151288092265)
XLA Ops:
  7.9 82.3 %all-gather.2.cloned.1.call-done = bf16[512,2048]{1,0:T(8,128)(2,1)} async-done(((bf16[16,2048]{1,0:T(8,128)(2,1)}), bf16[512,2048]{1,0:T(8,128)(2,1)}) %all-gather.2.cloned.1.call-update) | async-done | bytes 2097168 | tf_op jit(solution)/shard_map/all_gather | solution.py:33
  90.2 4.6 %fusion.63 = f32[512,512]{0,1:T(8,128)} fusion(bf16[512,2048]{1,0:T(8,128)(2,1)} %all-gather.2.cloned.1.call-done), kind=kOutput, calls=%fused_computation.104 | convolution fusion | flops 1073741824 | bytes 3145728 | tf_op jit(solution)/shard_map/dot_general | solution.py:42
  94.8 3.7 %fusion.64 = f32[1024,512]{1,0:T(8,128)} fusion(bf16[1024,2048]{1,0:T(8,128)(2,1)S(1)} %copy-done.5, bf16[512,2048]{1,0:T(8,128)(2,1)S(1)} %copy-done.6), kind=kOutput, calls=%fused_computation.105 | convolution fusion | flops 2147483648 | bytes 8388608 | tf_op jit(solution)/shard_map/dot_general | solution.py:39
  100.0 7.7 %all-to-all-start = ((bf16[32,2,512]{2,1,0:T(2,128)(2,1)}), bf16[32,2,512]{2,1,0:T(2,128)(2,1)S(1)}, u32[]{:S(2)}, u32[]{:S(2)}) async-start(bf16[32,2,512]{2,1,0:T(2,128)(2,1)} %reshape.86), calls=%async_computation | async-start | bytes 131072 | tf_op jit(solution)/shard_map/all_to_all | solution.py:35
  107.8 8.2 %all-to-all-done = bf16[32,2,512]{2,1,0:T(2,128)(2,1)S(1)} async-done(((bf16[32,2,512]{2,1,0:T(2,128)(2,1)}), bf16[32,2,512]{2,1,0:T(2,128)(2,1)S(1)}, u32[]{:S(2)}, u32[]{:S(2)}) %all-to-all-start) | async-done | bytes 65568 | tf_op jit(solution)/shard_map/all_to_all | solution.py:35
  116.2 55.4 %all-reduce.4.cloned.1.call-done = (f32[1024,512]{1,0:T(8,128)}, f32[512,512]{0,1:T(8,128)}) async-done(((f32[1024,512]{1,0:T(8,128)}, f32[512,512]{0,1:T(8,128)}), (f32[1024,512]{1,0:T(8,128)}, f32[512,512]{0,1:T(8,128)})) %all-reduce.4.cloned.1.call-update) | async-done | bytes 3145744 | tf_op jit(solution)/shard_map/psum | solution.py:50
  171.6 2.1 add_subtract_fusion
  174.9 11.7 %cholesky.103 = f32[128,128]{1,0:T(8,128)S(1)} custom-call(f32[128,128]{1,0:T(8,128)S(1)} %cholesky.263), custom_call_target="Cholesky" | custom-call | tf_op jit(solution)/shard_map/jit(cholesky)/cholesky | solution.py:51
  186.7 9.8 %custom-call.34 = f32[1,128,128]{1,2,0:T(8,128)S(1)} custom-call(f32[1,128,128]{2,1,0:T(8,128)S(1)} %get-tuple-element.34), custom_call_target="InvertDiagBlocksLowerTriangular" | custom-call | tf_op jit(solution)/shard_map/jit(cholesky)/cholesky | solution.py:51
  197.2 23.3 %cholesky.215 = f32[128,128]{1,0:T(8,128)S(1)} custom-call(f32[128,128]{1,0:T(8,128)S(1)} %cholesky.267), custom_call_target="Cholesky" | custom-call | tf_op jit(solution)/shard_map/jit(cholesky)/cholesky | solution.py:51
  220.8 9.8 %custom-call.35 = f32[1,128,128]{1,2,0:T(8,128)S(1)} custom-call(f32[1,128,128]{2,1,0:T(8,128)S(1)} %get-tuple-element.32), custom_call_target="InvertDiagBlocksLowerTriangular" | custom-call | tf_op jit(solution)/shard_map/jit(cholesky)/cholesky | solution.py:51
  231.7 11.7 %cholesky.236 = f32[128,128]{1,0:T(8,128)S(1)} custom-call(f32[128,128]{1,0:T(8,128)S(1)} %cholesky.272), custom_call_target="Cholesky" | custom-call | tf_op jit(solution)/shard_map/jit(cholesky)/cholesky | solution.py:51
  243.6 9.8 %custom-call.36 = f32[1,128,128]{1,2,0:T(8,128)S(1)} custom-call(f32[1,128,128]{2,1,0:T(8,128)S(1)} %get-tuple-element.30), custom_call_target="InvertDiagBlocksLowerTriangular" | custom-call | tf_op jit(solution)/shard_map/jit(cholesky)/cholesky | solution.py:51
  254.2 11.7 %cholesky.253 = f32[128,128]{1,0:T(8,128)S(1)} custom-call(f32[128,128]{1,0:T(8,128)S(1)} %convolution_subtract_fusion.8), custom_call_target="Cholesky" | custom-call | tf_op jit(solution)/shard_map/jit(cholesky)/cholesky | solution.py:51
  270.5 10.6 %while.1 = (s32[]{:T(128)}, f32[512,512]{0,1:T(8,128)S(1)}, s32[4,2]{0,1:T(2,128)S(1)}, f32[4,128,128]{2,1,0:T(8,128)}, s32[]{:T(128)}) while((s32[]{:T(128)}, f32[512,512]{0,1:T(8,128)S(1)}, s32[4,2]{0,1:T(2,128)S(1)}, f32[4,128,128]{2,1,0:T(8,128)}, s32[]{:T(128)}) %tuple.32), condition=%wide.while_cond, body=%wide.while_body.sunk | while | flops 2 | bytes 393829 | solution.py:23
  271.1 1.3 dynamic-slice.12
  273.8 1.3 dynamic-slice.12
  276.4 1.3 dynamic-slice.12
  279.1 1.3 dynamic-slice.12
  281.1 40.3 %custom-call.37 = f32[4,128,128]{1,2,0:T(8,128)S(1)} custom-call(f32[4,128,128]{2,1,0:T(8,128)} %get-tuple-element.9), custom_call_target="InvertDiagBlocksLowerTriangular" | custom-call | tf_op jit(solution)/shard_map/jit(_solve_triangular)/triangular_solve | solution.py:23
  323.6 3.0 subtract_bitcast_fusion
  328.9 1.8 convolution_subtract_fusion
  331.4 2.8 fusion.6
  335.8 2.2 convolution_subtract_fusion.2
  (92 shorter events, 21.7 us)
Async XLA Ops:
  7.2 83.0 %all-gather.2.cloned.1.call-start = ((), (), s32[]{:S(2)}) async-start(), calls=%async_computation.1 | async-start | bytes 2162688 | tf_op jit(solution)/shard_map/all_gather | solution.py:33
  7.9 163.7 %all-reduce.4.cloned.1.call-start = ((), (), s32[]{:S(2)}) async-start(), calls=%async_computation.2 | async-start | bytes 6291456 | tf_op jit(solution)/shard_map/psum | solution.py:50
  90.2 4.6 %copy-start.5 = (bf16[1024,2048]{1,0:T(8,128)(2,1)S(1)}, bf16[1024,2048]{1,0:T(8,128)(2,1)}, u32[]{:S(2)}) copy-start(bf16[1024,2048]{1,0:T(8,128)(2,1)} %param.8) | copy-start | bytes 12582916
  90.2 4.6 %copy-start.6 = (bf16[512,2048]{1,0:T(8,128)(2,1)S(1)}, bf16[512,2048]{1,0:T(8,128)(2,1)}, u32[]{:S(2)}) copy-start(bf16[512,2048]{1,0:T(8,128)(2,1)} %all-gather.2.cloned.1.call-done) | copy-start | bytes 6291460
  98.5 0.7 copy-start.3
  98.5 9.2 %copy-start.4 = (s32[2,512]{1,0:T(2,128)S(1)}, s32[2,512]{1,0:T(2,128)}, u32[]{:S(2)}) copy-start(s32[2,512]{1,0:T(2,128)} %param.7) | copy-start | bytes 12292
  98.5 9.2 %copy-start.2 = (s32[2,1024]{1,0:T(2,128)S(1)}, s32[2,1024]{1,0:T(2,128)}, u32[]{:S(2)}) copy-start(s32[2,1024]{1,0:T(2,128)} %param.6) | copy-start | bytes 24580
  100.0 16.0 %all-to-all-start = ((bf16[32,2,512]{2,1,0:T(2,128)(2,1)}), bf16[32,2,512]{2,1,0:T(2,128)(2,1)S(1)}, u32[]{:S(2)}, u32[]{:S(2)}) async-start(bf16[32,2,512]{2,1,0:T(2,128)(2,1)} %reshape.86), calls=%async_computation | async-start | bytes 131072 | tf_op jit(solution)/shard_map/all_to_all | solution.py:35
  116.2 57.9 %copy-start.1 = (bf16[32,16,64]{2,1,0:T(8,128)(2,1)}, bf16[32,16,64]{2,1,0:T(8,128)(2,1)S(1)}, u32[]{:S(2)}) copy-start(bf16[32,16,64]{2,1,0:T(8,128)(2,1)S(1)} %reshape.87) | copy-start | bytes 196612
  171.6 2.5 copy-start
  270.3 51.0 %slice-start = ((bf16[32,16,64]{2,1,0:T(8,128)(2,1)}), bf16[8,16,64]{2,1,0:T(8,128)(2,1)S(1)}, s32[]{:S(2)}) async-start(bf16[32,16,64]{2,1,0:T(8,128)(2,1)} %copy-done.1), calls=%async_computation.3 | async-start | bytes 65536 | tf_op jit(solution)/shard_map/jit(_solve_triangular)/triangular_solve | solution.py:26
  334.9 0.9 copy-start.7
Sparse Core Ops, SparseCore 0:
  10.6 79.6 all-gather.1
  98.7 72.8 all-reduce.3
